TPU v7x, 512 devices: a whole 4x8x8 slice. The times are simulated.
512 devices in a mesh: seq: 64 (over z, x, core), head: 8 (over y).
Axes of the slice: x: 4, y: 8, z: 8, core: 2. Of those that a mesh axis runs over, the one named last changes fastest.
Arguments:
- queries: bfloat16 [64, 16384, 128], P('head', 'seq'), may hold values from -1.25 to 1.25
- key_rows: bfloat16 [64, 16384, 128], P('head', 'seq'), may hold values from -1.25 to 1.25
- value_rows: bfloat16 [64, 16384, 128], P('head', 'seq'), may hold values from -1.25 to 1.25
- grad_out: bfloat16 [64, 16384, 128], P('head', 'seq'), may hold values from -1.25 to 1.25
Outputs:
- grad_query: bfloat16 [64, 16384, 128], P('head', 'seq')
- grad_key: bfloat16 [64, 16384, 128], P('head', 'seq')
- grad_value: bfloat16 [64, 16384, 128], P('head', 'seq')
All inputs are finite; a program needn't handle non-finite values.
Results may differ from a plain program's by a relative error of at most 0.0049.
Values sent between devices are 32-bit elements; how exact they have to be, the bound alone decides.
A program may use at most 192 MiB of HBM per device.

v0:
```python
import jax
import jax.numpy as jnp
from jax import lax
from jax.sharding import PartitionSpec as P

TILE = 256


def entering(x, axis, combine, identity, reverse):
    count, place = (lax.axis_size(axis), lax.axis_index(axis))
    everything = lax.all_gather(x, axis)
    start = jnp.broadcast_to(jnp.asarray(identity, x.dtype), x.shape)

    def turn(k, before):
        at = count - 1 - k if reverse else k
        reached = at > place if reverse else at < place
        new = combine(before, everything[at])
        return jnp.where(reached, new, before)

    return lax.fori_loop(0, count, turn, start)


def add_states(earlier, latter):
    return earlier + latter


def body(queries, key_rows, value_rows, grad_out):
    head_count, tokens, head_width = queries.shape
    tile_count = tokens // TILE
    tile_shape = (head_count, tile_count, TILE, head_width)
    query_tiles = queries.reshape(tile_shape)
    key_tiles = key_rows.reshape(tile_shape)
    value_tiles = value_rows.reshape(tile_shape)
    grad_tiles = grad_out.reshape(tile_shape)
    key_state = jnp.einsum(
        "hjsa,hjsb->hjab", key_tiles, value_tiles, preferred_element_type=jnp.float32
    )
    query_state = jnp.einsum(
        "hjta,hjtb->hjab", query_tiles, grad_tiles, preferred_element_type=jnp.float32
    )
    local_keys = jnp.sum(key_state, 1)
    local_queries = jnp.sum(query_state, 1)
    blank_state = jnp.zeros_like(local_keys)
    incoming = entering(local_keys, "seq", add_states, blank_state, False)
    outgoing = entering(local_queries, "seq", add_states, blank_state, True)
    zero_state = jnp.zeros((head_count, 1, head_width, head_width), jnp.float32)
    earlier_states = incoming[:, None] + jnp.concatenate(
        [zero_state, jnp.cumsum(key_state, 1)[:, :-1]], 1
    )
    later_states = outgoing[:, None] + jnp.concatenate(
        [jnp.cumsum(query_state[:, ::-1], 1)[:, ::-1][:, 1:], zero_state], 1
    )
    earlier_states = earlier_states.astype(jnp.bfloat16)
    later_states = later_states.astype(jnp.bfloat16)
    causal = (jnp.arange(TILE)[:, None] >= jnp.arange(TILE)[None, :])[None, None]
    out_scores = jnp.einsum(
        "hjta,hjsa->hjts", grad_tiles, value_tiles, preferred_element_type=jnp.float32
    )
    out_scores = jnp.where(causal, out_scores, 0.0).astype(jnp.bfloat16)
    attn_scores = jnp.einsum(
        "hjta,hjsa->hjts", query_tiles, key_tiles, preferred_element_type=jnp.float32
    )
    attn_scores = jnp.where(causal, attn_scores, 0.0).astype(jnp.bfloat16)
    grad_query = jnp.einsum(
        "hjts,hjsa->hjta", out_scores, key_tiles, preferred_element_type=jnp.float32
    )
    grad_query = grad_query + jnp.einsum(
        "hjtb,hjab->hjta", grad_tiles, earlier_states, preferred_element_type=jnp.float32
    )
    grad_key = jnp.einsum(
        "hjts,hjta->hjsa", out_scores, query_tiles, preferred_element_type=jnp.float32
    )
    grad_key = grad_key + jnp.einsum(
        "hjsb,hjab->hjsa", value_tiles, later_states, preferred_element_type=jnp.float32
    )
    grad_value = jnp.einsum(
        "hjts,hjtb->hjsb", attn_scores, grad_tiles, preferred_element_type=jnp.float32
    )
    grad_value = grad_value + jnp.einsum(
        "hjsa,hjab->hjsb", key_tiles, later_states, preferred_element_type=jnp.float32
    )
    flat_shape = (head_count, tokens, head_width)
    return (
        grad_query.astype(jnp.bfloat16).reshape(flat_shape),
        grad_key.astype(jnp.bfloat16).reshape(flat_shape),
        grad_value.astype(jnp.bfloat16).reshape(flat_shape),
    )


def solution(mesh):
    placed = (
        P("head", "seq", None),
        P("head", "seq", None),
        P("head", "seq", None),
        P("head", "seq", None),
    )
    return jax.shard_map(
        body,
        mesh=mesh,
        in_specs=placed,
        out_specs=(P("head", "seq", None), P("head", "seq", None), P("head", "seq", None)),
        check_vma=False,
    )
```

profile of v0, /device:TPU:1, one launch (start us, length us, event | category | flops | bytes accessed | tf_op | source)
XLA Modules:
  0.0 404.7 jit_solution(4933383181612335393)
XLA Ops:
  8.2 2.2 fusion.16
  12.2 1.5 fusion.15
  14.1 151.6 %all-gather.7.cloned.1.call-done = f32[512,128,128]{2,1,0:T(8,128)} async-done(((f32[8,128,128]{2,1,0:T(8,128)}), f32[512,128,128]{2,1,0:T(8,128)}) %all-gather.7.cloned.1.call-update) | async-done | bytes 33554448 | tf_op jit(solution)/shard_map/all_gather | solution.py:11
  165.7 81.3 %while.31 = (s32[]{:T(128)}, f32[8,128,128]{2,1,0:T(8,128)S(1)}, s32[]{:T(128)}, f32[64,8,128,128]{3,2,1,0:T(8,128)}, s32[]{:T(128)}, /*index=5*/s32[]{:T(128)}, s32[]{:T(128)}, s32[]{:T(128)}) while((s32[]{:T(128)}, f32[8,128,128]{2,1,0:T(8,128)S(1)}, s32[]{:T(128)}, f32[64,8,128,128]{3,2,1,0:T(8,128)}, s32[]{:T(128)}, ...), condition=%wide.region_3.4_spmd.clone, body=%wide.region_2.3_spmd.clone.sunk | while | flops 393224 | bytes 1573019 | solution.py:20
  179.5 1.3 add_select_fusion.5
  180.8 1.3 add_select_fusion.5
  182.1 1.3 add_select_fusion.5
  188.4 1.2 add_select_fusion.5
  189.7 1.2 add_select_fusion.5
  191.0 1.2 add_select_fusion.5
  192.2 1.2 add_select_fusion.5
  194.7 1.2 add_select_fusion.5
  196.0 1.2 add_select_fusion.5
  198.5 1.2 add_select_fusion.5
  199.8 1.2 add_select_fusion.5
  202.3 1.2 add_select_fusion.5
  206.1 1.2 add_select_fusion.5
  223.7 1.4 add_select_fusion.5
  225.1 1.4 add_select_fusion.5
  231.6 1.3 add_select_fusion.5
  232.9 1.2 add_select_fusion.5
  234.2 1.2 add_select_fusion.5
  235.5 1.2 add_select_fusion.5
  239.3 1.2 add_select_fusion.5
  240.5 1.2 add_select_fusion.5
  244.3 1.4 add_select_fusion.5
  245.7 1.2 add_select_fusion.5
  247.0 1.3 convolution_bitcast_fusion
  249.8 64.0 %all-gather.5.cloned.1.call-done = f32[512,128,128]{2,1,0:T(8,128)} async-done(((f32[8,128,128]{2,1,0:T(8,128)}), f32[512,128,128]{2,1,0:T(8,128)}) %all-gather.5.cloned.1.call-update) | async-done | bytes 33554448 | tf_op jit(solution)/shard_map/all_gather | solution.py:11
  313.9 80.1 %while.30 = (s32[]{:T(128)}, f32[8,128,128]{2,1,0:T(8,128)S(1)}, s32[]{:T(128)}, f32[64,8,128,128]{3,2,1,0:T(8,128)}, s32[]{:T(128)}, /*index=5*/s32[]{:T(128)}) while((s32[]{:T(128)}, f32[8,128,128]{2,1,0:T(8,128)S(1)}, s32[]{:T(128)}, f32[64,8,128,128]{3,2,1,0:T(8,128)}, s32[]{:T(128)}, /*index=5*/s32[]{:T(128)}) %tuple.81), condition=%wide.region_1.0_spmd.clone, body=%wide.region_0.0_spmd.clone.sunk | while | flops 393220 | bytes 1572957 | solution.py:20
  313.9 1.3 add_select_fusion.4
  394.0 2.7 fusion.4
  (130 shorter events, 133.4 us)
Async XLA Ops:
  7.2 1.0 copy-start
  7.2 3.3 copy-start.3
  7.2 3.3 copy-start.1
  7.2 158.5 %all-gather.7.cloned.1.call-start = ((), (), s32[]{:S(2)}) async-start(), calls=%async_computation.1 | async-start | bytes 34078720 | tf_op jit(solution)/shard_map/all_gather | solution.py:11
  10.4 1.8 copy-start.5
  10.4 303.4 %all-gather.5.cloned.1.call-start = ((), (), s32[]{:S(2)}) async-start(), calls=%async_computation | async-start | bytes 34078720 | tf_op jit(solution)/shard_map/all_gather | solution.py:11
  247.0 1.3 copy-start.2
  247.0 1.7 copy-start.4
  313.9 80.1 %copy-start.6 = (bf16[8,256,128]{2,1,0:T(8,128)(2,1)S(1)}, bf16[8,256,128]{2,1,0:T(8,128)(2,1)}, u32[]{:S(2)}) copy-start(bf16[8,256,128]{2,1,0:T(8,128)(2,1)} %param.8) | copy-start | bytes 1572868
Sparse Core Ops, SparseCore 0:
  11.9 153.7 all-gather.6
  169.6 144.2 all-gather.4
where the time goes:
time: 411 us; the launch traced here: 405 us
  waiting for transfers between devices  216 us (53%)
  other arithmetic  158 us (38%)
  between operations  14.2 us (3%)
  matrix products  11.9 us (3%)
    all_gather x2, waiting for transfers between devices, entering(): everything = lax.all_gather(x, axis)  216 us
    select_n x128, other arithmetic, turn(): return jnp.where(reached, new, before)  158 us
  transfers between devices with their start and end apart: 2, of which 2 were waited for; matrix products, arithmetic and copies ran while one was open for 21% of the time, Pallas kernels for 0%

commit v1 on v0

v1 whole, which is shorter than its diff:
```python
import jax
import jax.numpy as jnp
from jax import lax
from jax.experimental import pallas as pl
from jax.experimental.pallas import tpu as pltpu
from jax.sharding import PartitionSpec as P

ROWS, COLS = 8, 4
CHUNKS = 4
F32, BF16 = jnp.float32, jnp.bfloat16
NN = (((1,), (0,)), ((), ()))
NT = (((1,), (1,)), ((), ()))
TN = (((0,), (0,)), ((), ()))


def dot(a, b, dims):
    return lax.dot_general(a, b, dims, preferred_element_type=F32)


def kernel(
    q_hbm, k_hbm, v_hbm, g_hbm,
    gq_hbm, gk_hbm, gv_hbm,
    inb, part, outb, state, core_in, chip, side_in, far_src, far_in, total, z_src, z_in,
    far_out_src, far_out, side_out_src, side_out, core_out_src, core_out,
    in_sem, out_sem,
    ci_s, ci_r, si_s, si_r, fi_s, fi_r, z_s, z_r, fo_s, fo_r, so_s, so_r, co_s, co_r,
):
    tile = inb.shape[3]
    width = inb.shape[4]
    rows = width // CHUNKS
    place = lax.axis_index("seq")
    c = lax.rem(place, 2)
    x = lax.rem(lax.div(place, 2), COLS)
    z = lax.div(place, 2 * COLS)
    o = 1 - c
    odd = lax.rem(x, 2)
    right = lax.div(x, 2)
    xa = x + 1 - 2 * odd
    xb = COLS - 1 - x

    def device(zz, xx, cc):
        return {"seq": (zz * COLS + xx) * 2 + cc}

    core, side, far = device(z, x, o), device(z, xa, c), device(z, xb, c)
    up, down = lax.rem(z + 1, ROWS), lax.rem(z + ROWS - 1, ROWS)

    loads = []
    for slot, parity in ((0, o), (1, c)):
        for i, source in ((1, k_hbm), (2, v_hbm), (0, q_hbm), (3, g_hbm)):
            copy = pltpu.make_async_copy(source.at[:, parity], inb.at[i, slot], in_sem.at[i, slot])
            copy.start()
            loads.append(copy)

    barrier = pltpu.get_barrier_semaphore()
    for peer in (core, side, far, device(up, x, c), device(down, x, c)):
        pl.semaphore_signal(barrier, inc=1, device_id=peer, device_id_type=pl.DeviceIdType.MESH)

    order = (COLS - 1 - xa, xa, COLS - 1 - x, x)

    def remote(src, dst, send, recv, peer):
        return pltpu.make_async_remote_copy(
            src_ref=src, dst_ref=dst, send_sem=send, recv_sem=recv, device_id=peer,
            device_id_type=pl.DeviceIdType.MESH,
        )

    sends = []

    def core_copy(w, j):
        return remote(state.at[w, 0, j], core_in.at[w, j], ci_s.at[w, j], ci_r.at[w, j], core)

    def side_copy(w, n, j):
        return remote(chip.at[w, j], side_in.at[w, n], si_s.at[w, n], si_r.at[w, n], side)

    def far_copy(w):
        return remote(far_src.at[w], far_in.at[w], fi_s.at[w], fi_r.at[w], far)

    def part_of(k):
        return pl.ds(k * rows, rows)

    def z_copy(w, k):
        peer = device(lax.rem(z + 1 - 2 * w + ROWS, ROWS), x, c)
        return remote(z_src.at[w, part_of(k)], z_in.at[w, part_of(k)], z_s.at[w, k], z_r.at[w, k], peer)

    def far_back(w, k):
        return remote(far_out_src.at[w, part_of(k)], far_out.at[w, part_of(k)], fo_s.at[w, k], fo_r.at[w, k], far)

    def side_back(w, n):
        return remote(side_out_src.at[w, n], side_out.at[w, n], so_s.at[w, n], so_r.at[w, n], side)

    def core_back(w, j):
        return remote(core_out_src.at[w, j], core_out.at[w, j], co_s.at[w, j], co_r.at[w, j], core)

    def start(copy):
        copy.start()
        sends.append(copy)

    def make_state(w, slot, j):
        a, b = ((1, 2), (0, 3))[w]
        state[w, slot, j] = dot(inb[a, slot, j], inb[b, slot, j], TN)

    for copy in loads[:4]:
        copy.wait()
    for n, j in enumerate(order):
        for w in (0, 1):
            make_state(w, 0, j)
        if n == 0:
            pl.semaphore_wait(barrier, 5)
        for w in (0, 1):
            start(core_copy(w, j))
    for copy in loads[4:]:
        copy.wait()
    for j in order:
        for w in (0, 1):
            make_state(w, 1, j)

    for n, j in enumerate(order):
        for w in (0, 1):
            core_copy(w, j).wait_recv()
            chip[w, j] = state[w, 1, j] + core_in[w, j]
            if n < 2:
                start(side_copy(w, n, j))

    causal = lax.broadcasted_iota(jnp.int32, (tile, tile), 0) >= lax.broadcasted_iota(jnp.int32, (tile, tile), 1)

    def local(slot):
        @pl.loop(0, COLS)
        def _(j):
            q, k, v, g = (inb[i, slot, j] for i in range(4))
            scores = jnp.where(causal, dot(g, v, NT), 0.0).astype(BF16)
            part[0, slot, j] = dot(scores, k, NN)
            part[1, slot, j] = dot(scores, q, TN)
            scores = jnp.where(causal, dot(q, k, NT), 0.0).astype(BF16)
            part[2, slot, j] = dot(scores, g, TN)

    local(0)
    for w in (0, 1):
        side_copy(w, 0, x).wait_recv()
        far_src[w] = chip[w, COLS - 1 - x] + side_in[w, 0]
        start(far_copy(w))
    local(1)
    for w in (0, 1):
        side_copy(w, 1, x).wait_recv()
        total[w] = chip[w, x] + side_in[w, 1]

    late = lax.div(z, ROWS // 2)
    kinds = [lax.rem(t + late, 2) for t in (0, 1)]
    for w in (0, 1):
        far_copy(w).wait_recv()

    def flag(value):
        return value.astype(F32)

    for w in kinds:
        at = z + w * (ROWS - 1 - 2 * z)
        own_base = flag(right + w * (1 - 2 * right))
        far_base = 1.0 - own_base
        side_self = flag(odd + w * (1 - 2 * odd))
        side_other = 1.0 - side_self

        @pl.when(at == 0)
        def _():
            z_in[w] = jnp.zeros((width, width), F32)

        for k in range(CHUNKS):
            span = part_of(k)

            @pl.when(at > 0)
            def _():
                z_copy(w, k).wait_recv()

            before = z_in[w, span]
            ours = total[w, span]
            theirs = far_in[w, span]

            @pl.when(at < ROWS - 1)
            def _():
                z_src[w, span] = before + (ours + theirs)
                z_copy(w, k).start()

            far_out_src[w, span] = before + far_base * ours
            start(far_back(w, k))
            base = before + own_base * theirs
            side_out_src[w, 1, span] = base + side_other * chip[w, x, span]
            side_out[w, 2, span] = base + side_self * side_in[w, 1, span]
        start(side_back(w, 1))

    core_other = [flag(c + w * (1 - 2 * c)) for w in (0, 1)]

    def hand_over(w, j, offset):
        partner = 1.0 - flag(c + w * (1 - 2 * c))
        core_out_src[w, j] = offset + partner * state[w, 1, j]
        start(core_back(w, j))
        core_out[w, COLS + j] = offset + (1.0 - partner) * core_in[w, j]

    for w in kinds:
        for k in range(CHUNKS):
            far_back(w, k).wait_recv()
        side_self = flag(odd + w * (1 - 2 * odd))
        base = far_out[w]
        side_out_src[w, 0] = base + (1.0 - side_self) * chip[w, COLS - 1 - x]
        start(side_back(w, 0))
        side_out[w, 3] = base + side_self * side_in[w, 0]
        hand_over(w, x, side_out[w, 2])
        hand_over(w, COLS - 1 - x, side_out[w, 3])
    for w in kinds:
        for n, j in ((1, xa), (0, COLS - 1 - xa)):
            side_back(w, n).wait_recv()
            hand_over(w, j, side_out[w, n])

    def finish(slot, parity, j, earlier, later):
        earlier, later = earlier.astype(BF16), later.astype(BF16)
        outb[0, slot, j] = (part[0, slot, j] + dot(inb[3, slot, j], earlier, NT)).astype(BF16)
        outb[1, slot, j] = (part[1, slot, j] + dot(inb[2, slot, j], later, NT)).astype(BF16)
        outb[2, slot, j] = (part[2, slot, j] + dot(inb[1, slot, j], later, NN)).astype(BF16)
        for i, target in enumerate((gq_hbm, gk_hbm, gv_hbm)):
            pltpu.make_async_copy(outb.at[i, slot, j], target.at[j, parity], out_sem.at[i, slot, j]).start()

    order = (x, COLS - 1 - x, xa, COLS - 1 - xa)
    for j in order:
        finish(1, c, j, core_out[0, COLS + j], core_out[1, COLS + j])
    for j in order:
        for w in (0, 1):
            core_back(w, j).wait_recv()
        finish(0, o, j, core_out[0, j], core_out[1, j])

    for copy in sends:
        copy.wait_send()
    for w in kinds:
        at = z + w * (ROWS - 1 - 2 * z)

        @pl.when(at < ROWS - 1)
        def _():
            for k in range(CHUNKS):
                z_copy(w, k).wait_send()

    for slot, parity in ((1, c), (0, o)):
        for j in range(COLS):
            for i, target in enumerate((gq_hbm, gk_hbm, gv_hbm)):
                pltpu.make_async_copy(outb.at[i, slot, j], target.at[j, parity], out_sem.at[i, slot, j]).wait()


def body(queries, key_rows, value_rows, grad_out):
    heads, tile, width = queries.shape
    split = (heads // 2, 2, tile, width)
    square = (width, width)
    sem = pltpu.SemaphoreType.DMA
    half = heads // 2
    grads = pl.pallas_call(
        kernel,
        out_shape=[jax.ShapeDtypeStruct(split, BF16)] * 3,
        in_specs=[pl.BlockSpec(memory_space=pl.ANY)] * 4,
        out_specs=[pl.BlockSpec(memory_space=pl.ANY)] * 3,
        scratch_shapes=[
            pltpu.VMEM((4, 2, half, tile, width), BF16),
            pltpu.VMEM((3, 2, half, tile, width), F32),
            pltpu.VMEM((3, 2, half, tile, width), BF16),
            pltpu.VMEM((2, 2, half, *square), F32),
            pltpu.VMEM((2, half, *square), F32),
            pltpu.VMEM((2, half, *square), F32),
            pltpu.VMEM((2, 2, *square), F32),
            pltpu.VMEM((2, *square), F32),
            pltpu.VMEM((2, *square), F32),
            pltpu.VMEM((2, *square), F32),
            pltpu.VMEM((2, *square), F32),
            pltpu.VMEM((2, *square), F32),
            pltpu.VMEM((2, *square), F32),
            pltpu.VMEM((2, *square), F32),
            pltpu.VMEM((2, 2, *square), F32),
            pltpu.VMEM((2, 4, *square), F32),
            pltpu.VMEM((2, half, *square), F32),
            pltpu.VMEM((2, 2 * half, *square), F32),
            sem((4, 2)),
            sem((3, 2, half)),
            sem((2, half)), sem((2, half)),
            sem((2, 2)), sem((2, 2)),
            sem((2,)), sem((2,)),
            sem((2, CHUNKS)), sem((2, CHUNKS)),
            sem((2, CHUNKS)), sem((2, CHUNKS)),
            sem((2, 2)), sem((2, 2)),
            sem((2, half)), sem((2, half)),
        ],
        compiler_params=pltpu.CompilerParams(
            collective_id=0, has_side_effects=True, vmem_limit_bytes=48 * 2**20
        ),
    )(*(a.reshape(split) for a in (queries, key_rows, value_rows, grad_out)))
    return tuple(g.reshape(heads, tile, width) for g in grads)


def solution(mesh):
    placed = P("head", "seq", None)
    return jax.shard_map(
        body, mesh=mesh, in_specs=(placed,) * 4, out_specs=(placed,) * 3, check_vma=False
    )
```

time: 411 us -> 59.5 us (0.14)
  the two profiles are of different devices: /device:TPU:1 before, /device:TPU:56 now
where the time goes in v1:
time: 59.5 us; the launch traced here: 59.2 us
  Pallas kernels  52 us (87%)
  local copies, waits for them, and re-layouts  6.54 us (11%)
  between operations  0.65 us (1%)
    pallas_call x1, Pallas kernels, body(): pl.pallas_call(kernel, out_shape=[jax.ShapeDtypeStruct(split, BF16)] * 3,...  52 us
    unnamed x11, local copies, waits for them, and re-layouts  6.54 us

profile of v1, /device:TPU:56, one launch (start us, length us, event | category | flops | bytes accessed | tf_op | source)
XLA Modules:
  0.0 59.2 jit_solution(17287050130774608212)
XLA Ops:
  0.6 0.0 copy-start
  0.6 1.0 %copy-done = bf16[8,256,128]{2,1,0:T(8,128)(2,1)S(1)} copy-done((bf16[8,256,128]{2,1,0:T(8,128)(2,1)S(1)}, bf16[8,256,128]{2,1,0:T(8,128)(2,1)}, u32[]{:S(2)}) %copy-start) | copy-done | bytes 524312
  1.7 0.0 copy-start.1
  1.7 1.0 %copy-done.1 = bf16[8,256,128]{2,1,0:T(8,128)(2,1)S(1)} copy-done((bf16[8,256,128]{2,1,0:T(8,128)(2,1)S(1)}, bf16[8,256,128]{2,1,0:T(8,128)(2,1)}, u32[]{:S(2)}) %copy-start.1) | copy-done | bytes 524312
  2.7 0.0 copy-start.2
  2.7 1.0 %copy-done.2 = bf16[8,256,128]{2,1,0:T(8,128)(2,1)S(1)} copy-done((bf16[8,256,128]{2,1,0:T(8,128)(2,1)S(1)}, bf16[8,256,128]{2,1,0:T(8,128)(2,1)}, u32[]{:S(2)}) %copy-start.2) | copy-done | bytes 524312
  3.8 0.0 copy-start.3
  3.8 1.0 %copy-done.3 = bf16[8,256,128]{2,1,0:T(8,128)(2,1)S(1)} copy-done((bf16[8,256,128]{2,1,0:T(8,128)(2,1)S(1)}, bf16[8,256,128]{2,1,0:T(8,128)(2,1)}, u32[]{:S(2)}) %copy-start.3) | copy-done | bytes 524312
  4.8 52.0 %shard_map.67 = (bf16[4,2,256,128]{3,2,1,0:T(8,128)(2,1)S(1)}, bf16[4,2,256,128]{3,2,1,0:T(8,128)(2,1)S(1)}, bf16[4,2,256,128]{3,2,1,0:T(8,128)(2,1)S(1)}) custom-call(bf16[4,2,256,128]{3,2,1,0:T(8,128)(2,1)S(1)} %bitcast.10, bf16[4,2,256,128]{3,2,1,0:T(8,128)(2,1)S(1)} %bitcast.11, bf16[4,2,256,128]{3,2,1,0:T(8,128)(2,1)S(1)} %bitcast.12, ...), custom_call_target="tpu_custom_call" | custom-call | tf_op jit(solution)/shard_map/pallas_call | solution.py:248
  56.9 0.8 %copy.10 = bf16[8,256,128]{2,1,0:T(8,128)(2,1)} copy(bf16[8,256,128]{2,1,0:T(8,128)(2,1)S(1)} %bitcast.9) | data formatting | bytes 1048576
  57.7 0.8 %copy.11 = bf16[8,256,128]{2,1,0:T(8,128)(2,1)} copy(bf16[8,256,128]{2,1,0:T(8,128)(2,1)S(1)} %bitcast.8) | data formatting | bytes 1048576
  58.4 0.8 %copy.12 = bf16[8,256,128]{2,1,0:T(8,128)(2,1)} copy(bf16[8,256,128]{2,1,0:T(8,128)(2,1)S(1)} %bitcast.7) | data formatting | bytes 1048576
Async XLA Ops:
  0.6 1.0 %copy-start = (bf16[8,256,128]{2,1,0:T(8,128)(2,1)S(1)}, bf16[8,256,128]{2,1,0:T(8,128)(2,1)}, u32[]{:S(2)}) copy-start(bf16[8,256,128]{2,1,0:T(8,128)(2,1)} %param.4) | copy-start | bytes 1572868
  1.7 1.0 %copy-start.1 = (bf16[8,256,128]{2,1,0:T(8,128)(2,1)S(1)}, bf16[8,256,128]{2,1,0:T(8,128)(2,1)}, u32[]{:S(2)}) copy-start(bf16[8,256,128]{2,1,0:T(8,128)(2,1)} %param.5) | copy-start | bytes 1572868
  2.7 1.0 %copy-start.2 = (bf16[8,256,128]{2,1,0:T(8,128)(2,1)S(1)}, bf16[8,256,128]{2,1,0:T(8,128)(2,1)}, u32[]{:S(2)}) copy-start(bf16[8,256,128]{2,1,0:T(8,128)(2,1)} %param.6) | copy-start | bytes 1572868
  3.8 1.0 %copy-start.3 = (bf16[8,256,128]{2,1,0:T(8,128)(2,1)S(1)}, bf16[8,256,128]{2,1,0:T(8,128)(2,1)}, u32[]{:S(2)}) copy-start(bf16[8,256,128]{2,1,0:T(8,128)(2,1)} %param.7) | copy-start | bytes 1572868

commit v2 on v0

v2 whole, which is shorter than its diff:
```python
import jax
import jax.numpy as jnp
from jax import lax
from jax.experimental import pallas as pl
from jax.experimental.pallas import tpu as pltpu
from jax.sharding import PartitionSpec as P

ROWS, COLS, PER = 8, 4, 2
HALF = ROWS // 2
F32, BF16 = jnp.float32, jnp.bfloat16
NN = (((1,), (0,)), ((), ()))
NT = (((1,), (1,)), ((), ()))
TN = (((0,), (0,)), ((), ()))


def dot(a, b, dims):
    return lax.dot_general(a, b, dims, preferred_element_type=F32)


def kernel(
    k_hbm, v_hbm, q_hbm, g_hbm,
    gq, gk, gv,
    inb, part, own, away, core_in, chip, row_in, ahead, rowsum, col_in, offset, half_src, half_in,
    row_src, row_out, core_src, core_out,
    in_sem,
    ci_s, ci_r, ri_s, ri_r, z_s, z_r, h_s, h_r, ro_s, ro_r, co_s, co_r, ready,
):
    tile, width = inb.shape[3:]
    place = lax.axis_index("seq")
    c = lax.rem(place, 2)
    x = lax.rem(lax.div(place, 2), COLS)
    z = lax.div(place, 2 * COLS)
    px = x + c * (COLS - 1 - 2 * x)
    p = z + c * (ROWS - 1 - 2 * z)
    g = lax.div(p, HALF)
    i = lax.rem(p, HALF)

    def device(pp, ppx):
        zz = pp + c * (ROWS - 1 - 2 * pp)
        xx = ppx + c * (COLS - 1 - 2 * ppx)
        return {"seq": (zz * COLS + xx) * 2 + c}

    partner = {"seq": place + 1 - 2 * c}

    def row_place(start, off):
        return lax.rem(start + off, COLS)

    loads = []
    for a, source in ((2, q_hbm), (3, g_hbm), (0, k_hbm), (1, v_hbm)):
        for n in range(2):
            span = pl.ds(n * 2, 2)
            copy = pltpu.make_async_copy(source.at[span], inb.at[a, span], in_sem.at[a, n])
            copy.start()
            loads.append(copy)

    barrier = pltpu.get_barrier_semaphore()

    def greet(peer):
        pl.semaphore_signal(barrier, inc=1, device_id=peer, device_id_type=pl.DeviceIdType.MESH)

    greet(partner)
    for off in (1, 2, 3):
        greet(device(p, row_place(px, off)))
    first = lax.rem(z, HALF)
    for d in range(HALF):
        @pl.when(d > first)
        def _():
            zz = z - first + d
            greet({"seq": (zz * COLS + x) * 2 + c})

    for low, high, core in ((0, 7, 0), (0, 6, 0), (3, 4, 0), (3, 5, 0), (0, 7, 1), (1, 7, 1), (3, 4, 1), (2, 4, 1)):
        @pl.when((z == low) & (c == core))
        def _():
            greet({"seq": (high * COLS + x) * 2 + core})

    upper = lax.div(z, HALF)
    ends = jnp.where((z == 7) | (z == 4), 2, 0)
    expected = 4 + first + jnp.where(c == 0, upper, ends)

    def remote(src, dst, send, recv, peer):
        return pltpu.make_async_remote_copy(
            src_ref=src, dst_ref=dst, send_sem=send, recv_sem=recv, device_id=peer,
            device_id_type=pl.DeviceIdType.MESH,
        )

    sends = []

    def start(copy):
        copy.start()
        sends.append(copy)

    def core_copy(j, u):
        return remote(away.at[j, u], core_in.at[j, u], ci_s.at[j, u], ci_r.at[j, u], partner)

    def row_copy(off, u):
        j = row_place(px, off)
        return remote(chip.at[j, u], row_in.at[px, u], ri_s.at[off, u], ri_r.at[px, u], device(p, j))

    def col_copy(d, u):
        return remote(rowsum.at[u], col_in.at[i, u], z_s.at[d, u], z_r.at[i, u], device(g * HALF + d, px))

    def half_copy(to, n, u):
        return remote(half_src.at[u], half_in.at[u], h_s.at[n, u], h_r.at[u], device(to, px))

    def row_back(off, u):
        j = row_place(px, off)
        return remote(row_src.at[off, u], row_out.at[px, u], ro_s.at[off, u], ro_r.at[px, u], device(p, j))

    def core_back(j, u):
        return remote(core_src.at[j, u], core_out.at[j, u], co_s.at[j, u], co_r.at[j, u], partner)

    def arrival(ref, sem):
        return remote(ref, ref, sem, sem, partner)

    other_px = COLS - 1 - px
    for copy in loads:
        copy.wait()
    for u in range(PER):
        for off in (2, 1, 3, 0):
            j = row_place(other_px, off)
            kind = 2 * (1 - c)
            away[j, u] = dot(inb[kind, j, u], inb[kind + 1, j, u], TN)
            if u == 0 and off == 2:
                pl.semaphore_wait(barrier, expected)
            start(core_copy(j, u))

    def answer(sender):
        pl.semaphore_signal(
            ready.at[p], inc=1, device_id=device(sender, px), device_id_type=pl.DeviceIdType.MESH
        )

    for s in range(HALF):
        @pl.when((c == 0) & (s < i))
        def _():
            answer(g * HALF + s)

        @pl.when((c == 1) & (p == 0) & (s > 0))
        def _():
            answer(s)

    @pl.when((c == 0) & (g == 1))
    def _():
        answer(jnp.where(i < 2, HALF - 1, 0))

    for u in range(PER):
        for off in (2, 1, 3, 0):
            j = row_place(px, off)
            own[j, u] = dot(inb[2 * c, j, u], inb[2 * c + 1, j, u], TN)

    for u in range(PER):
        for off in (2, 1, 3, 0):
            j = row_place(px, off)
            core_copy(j, u).wait_recv()
            if off:
                chip[j, u] = own[j, u] + core_in[j, u]
                start(row_copy(off, u))
            else:
                row_in[px, u] = own[px, u] + core_in[px, u]

    causal = lax.broadcasted_iota(jnp.int32, (tile, tile), 0) >= lax.broadcasted_iota(jnp.int32, (tile, tile), 1)

    def local(half):
        @pl.loop(0, COLS)
        def _(n):
            j, u = half * 2 + lax.div(n, 2), lax.rem(n, 2)
            k, v, q, go = (inb[a, j, u] for a in range(4))
            scores = jnp.where(causal, dot(go, v, NT), 0.0).astype(BF16)
            part[0, j, u] = dot(scores, k, NN)
            part[1, j, u] = dot(scores, q, TN)
            scores = jnp.where(causal, dot(q, k, NT), 0.0).astype(BF16)
            part[2, j, u] = dot(scores, go, TN)

    local(0)
    lower_end = (g == 0) & ((i == 0) | (i == HALF - 1))

    for u in range(PER):
        for off in (1, 3, 2):
            j = row_place(px, off)
            arrival(row_in.at[j, u], ri_r.at[j, u]).wait_recv()
        total = row_in[0, u]
        ahead[0, u] = jnp.zeros((width, width), F32)
        ahead[1, u] = total
        total = total + row_in[1, u]
        ahead[2, u] = total
        total = total + row_in[2, u]
        ahead[3, u] = total
        rowsum[u] = total + row_in[3, u]
        for d in range(HALF):
            @pl.when((d > i) | ((g == 0) & (i > 0) & (d == 0)))
            def _():
                if u == 0:
                    @pl.when((c == 0) == (d > i))
                    def _():
                        pl.semaphore_wait(ready.at[g * HALF + d], 1)
                col_copy(d, u).start()

    @pl.when(g == 1)
    def _():
        local(1)

    for u in range(PER):
        offset[u] = jnp.zeros((width, width), F32)
        for s in range(HALF - 1):
            @pl.when(s < i)
            def _():
                arrival(col_in.at[s, u], z_r.at[s, u]).wait_recv()
                offset[u] += col_in[s, u]

        for end, targets in ((0, (7, 6)), (HALF - 1, (4, 5))):
            @pl.when((g == 0) & (i == end))
            def _():
                if end == 0:
                    for s in range(1, HALF):
                        arrival(col_in.at[s, u], z_r.at[s, u]).wait_recv()
                    half_src[u] = rowsum[u] + col_in[1, u] + col_in[2, u] + col_in[3, u]
                else:
                    half_src[u] = offset[u] + rowsum[u]
                for n, to in enumerate(targets):
                    if u == 0:
                        @pl.when(c == 0)
                        def _():
                            pl.semaphore_wait(ready.at[to], 1)
                    half_copy(to, n, u).start()

        @pl.when(g == 1)
        def _():
            arrival(half_in.at[u], h_r.at[u]).wait_recv()
            offset[u] += half_in[u]

        for off in (2, 1, 3):
            row_src[off, u] = offset[u] + ahead[row_place(px, off), u]
            start(row_back(off, u))
        row_out[px, u] = offset[u] + ahead[px, u]

    @pl.when(g == 0)
    def _():
        local(1)

    def emit(n, j, u, value):
        (gq, gk, gv)[n][j, u] = (part[n, j, u] + value).astype(BF16)

    def finish(kind, j, u, state):
        state = state.astype(BF16)

        @pl.when(kind == 0)
        def _():
            emit(0, j, u, dot(inb[3, j, u], state, NT))

        @pl.when(kind == 1)
        def _():
            emit(1, j, u, dot(inb[1, j, u], state, NT))
            emit(2, j, u, dot(inb[0, j, u], state, NN))

    def turn(n):
        m = lax.rem(n, COLS)
        return m + lax.div(m, 2) * (1 - 2 * lax.rem(m, 2)), lax.div(n, COLS)

    def own_kind():
        @pl.loop(0, COLS * PER)
        def _(n):
            off, u = turn(n)
            j = row_place(px, off)

            @pl.when(off > 0)
            def _():
                arrival(row_out.at[j, u], ro_r.at[j, u]).wait_recv()

            core_src[j, u] = row_out[j, u] + own[j, u]
            core_back(j, u).start()
            finish(c, j, u, row_out[j, u])

    def other_kind():
        @pl.loop(0, COLS * PER)
        def _(n):
            off, u = turn(n)
            j = row_place(other_px, off)
            core_back(j, u).wait_recv()
            finish(1 - c, j, u, core_out[j, u])

    @pl.when(g == 1)
    def _():
        other_kind()

    own_kind()

    @pl.when(g == 0)
    def _():
        other_kind()

    for copy in sends:
        copy.wait_send()
    for u in range(PER):
        for d in range(HALF):
            @pl.when((d > i) | ((g == 0) & (i > 0) & (d == 0)))
            def _():
                col_copy(d, u).wait_send()

        @pl.when(lower_end)
        def _():
            for n in range(2):
                half_copy(0, n, u).wait_send()

        for j in range(COLS):
            core_back(j, u).wait_send()


def put(*refs):
    sources, targets, sems = refs[:3], refs[3:6], refs[6]
    copies = [
        pltpu.make_async_copy(sources[n].at[j], targets[n].at[j], sems.at[n, j])
        for n in range(3)
        for j in range(COLS)
    ]
    for copy in copies:
        copy.start()
    for copy in copies:
        copy.wait()


def body(queries, key_rows, value_rows, grad_out):
    heads, tile, width = queries.shape
    split = (COLS, PER, tile, width)
    square = (width, width)
    sem = pltpu.SemaphoreType.DMA
    four = pltpu.VMEM((COLS, PER, *square), F32)
    two = pltpu.VMEM((PER, *square), F32)
    pairs = sem((COLS, PER))
    grads = pl.pallas_call(
        kernel,
        out_shape=[pltpu.VMEM(split, BF16)] * 3,
        in_specs=[pl.BlockSpec(memory_space=pl.ANY)] * 4,
        out_specs=[pl.BlockSpec(memory_space=pltpu.VMEM)] * 3,
        scratch_shapes=[
            pltpu.VMEM((4, *split), BF16),
            pltpu.VMEM((3, *split), F32),
            four, four, four, four, four, four, two, four, two, two, two,
            four, four, four, four,
            sem((4, 2)),
            pairs, pairs, pairs, pairs, pairs, pairs, sem((2, PER)), sem((PER,)), pairs, pairs, pairs, pairs,
            pltpu.SemaphoreType.REGULAR((ROWS,)),
        ],
        compiler_params=pltpu.CompilerParams(
            collective_id=0, has_side_effects=True, vmem_limit_bytes=61 * 2**20
        ),
    )(*(a.reshape(split) for a in (key_rows, value_rows, queries, grad_out)))
    grads = pl.pallas_call(
        put,
        out_shape=[jax.ShapeDtypeStruct(split, BF16)] * 3,
        in_specs=[pl.BlockSpec(memory_space=pl.ANY)] * 3,
        out_specs=[pl.BlockSpec(memory_space=pl.ANY)] * 3,
        scratch_shapes=[sem((3, COLS))],
        compiler_params=pltpu.CompilerParams(vmem_limit_bytes=2**20),
    )(*grads)
    return tuple(a.reshape(heads, tile, width) for a in grads)


def solution(mesh):
    placed = P("head", "seq", None)
    return jax.shard_map(
        body, mesh=mesh, in_specs=(placed,) * 4, out_specs=(placed,) * 3, check_vma=False
    )
```

time: 411 us -> 38.6 us (0.09); the launches traced: 405 us -> 38.5 us
  waiting for transfers between devices: 216 us -> 0 us
  other arithmetic: 158 us -> 0 us
  Pallas kernels: 0 us -> 37.9 us
  between operations: 14.2 us -> 0.64 us
  matrix products: 11.9 us -> 0 us
    all_gather x2 -> x0, waiting for transfers between devices: 216 us -> none  [entering(): everything = lax.all_gather(x, axis)]
    select_n x128 -> x0, other arithmetic: 158 us -> none  [turn(): return jnp.where(reached, new, before)]
    pallas_call x0 -> x2, Pallas kernels: none -> 37.9 us  [the longest x1 36.6 us: body(): pl.pallas_call(kernel, out_shape=[pltpu.VMEM(split, BF16)] * 3, in_specs=...]
    dot_general x9 -> x0, matrix products: 11.9 us -> none  [the longest x1 2.73 us: body(): jnp.einsum('hjts,hjtb->hjsb', attn_scores, grad_tiles, preferred_element_...]
  transfers between devices with their start and end apart: 2 -> 0, of which waited for: 2 -> 0; matrix products, arithmetic and copies ran while one was open for 21% -> 0% of each run, Pallas kernels for 0% -> 0%
where the time goes in v2:
time: 38.6 us; the launch traced here: 38.5 us
  Pallas kernels  37.9 us (98%)
  between operations  0.64 us (2%)
    pallas_call x1, Pallas kernels, body(): pl.pallas_call(kernel, out_shape=[pltpu.VMEM(split, BF16)] * 3, in_specs=...  36.6 us
    pallas_call x1, Pallas kernels, body(): pl.pallas_call(put, out_shape=[jax.ShapeDtypeStruct(split, BF16)] * 3, in...  1.24 us

profile of v2, /device:TPU:1, one launch (start us, length us, event | category | flops | bytes accessed | tf_op | source)
XLA Modules:
  0.0 38.5 jit_solution(13185272472043975341)
XLA Ops:
  0.6 36.6 %shard_map.67 = (bf16[4,2,256,128]{3,2,1,0:T(8,128)(2,1)S(1)}, bf16[4,2,256,128]{3,2,1,0:T(8,128)(2,1)S(1)}, bf16[4,2,256,128]{3,2,1,0:T(8,128)(2,1)S(1)}) custom-call(bf16[4,2,256,128]{3,2,1,0:T(8,128)(2,1)} %bitcast.7, bf16[4,2,256,128]{3,2,1,0:T(8,128)(2,1)} %bitcast.8, bf16[4,2,256,128]{3,2,1,0:T(8,128)(2,1)} %bitcast.9, bf16[4,2,256,128]{3,2,1,0:T(8,128)(2,1)} %bitcast.10), custom_call_target="tpu_custom_call" | custom-call | tf_op jit(solution)/shard_map/pallas_call | solution.py:328
  37.3 1.2 %shard_map.68 = (bf16[4,2,256,128]{3,2,1,0:T(8,128)(2,1)}, bf16[4,2,256,128]{3,2,1,0:T(8,128)(2,1)}, bf16[4,2,256,128]{3,2,1,0:T(8,128)(2,1)}) custom-call(bf16[4,2,256,128]{3,2,1,0:T(8,128)(2,1)S(1)} %get-tuple-element.9.refs_0_, bf16[4,2,256,128]{3,2,1,0:T(8,128)(2,1)S(1)} %get-tuple-element.10.refs_1_, bf16[4,2,256,128]{3,2,1,0:T(8,128)(2,1)S(1)} %get-tuple-element.11.refs_2_), custom_call_target="tpu_custom_call" | custom-call | tf_op jit(solution)/shard_map/pallas_call | solution.py:346

commit v3 on v2

v3 whole, which is shorter than its diff:
```python
import jax
import jax.numpy as jnp
from jax import lax
from jax.experimental import pallas as pl
from jax.experimental.pallas import tpu as pltpu
from jax.sharding import PartitionSpec as P

ROWS, COLS, PER = 8, 4, 2
HALF = ROWS // 2
F32, BF16 = jnp.float32, jnp.bfloat16
NN = (((1,), (0,)), ((), ()))
NT = (((1,), (1,)), ((), ()))
TN = (((0,), (0,)), ((), ()))


def dot(a, b, dims):
    return lax.dot_general(a, b, dims, preferred_element_type=F32)


def kernel(
    k_hbm, v_hbm, q_hbm, g_hbm,
    gq, gk, gv,
    inb, part, own, away, core_in, chip, row_in, ahead, rowsum, col_in, offset, half_src, half_in, pair_src,
    row_src, row_out, core_src, core_out,
    in_sem,
    ci_s, ci_r, ri_s, ri_r, z_s, z_r, h_s, h_r, ro_s, ro_r, co_s, co_r, ready, row_ready,
):
    tile, width = inb.shape[3:]
    place = lax.axis_index("seq")
    c = lax.rem(place, 2)
    x = lax.rem(lax.div(place, 2), COLS)
    z = lax.div(place, 2 * COLS)
    px = x + c * (COLS - 1 - 2 * x)
    p = z + c * (ROWS - 1 - 2 * z)
    g = lax.div(p, HALF)
    i = lax.rem(p, HALF)

    def device(pp, ppx):
        zz = pp + c * (ROWS - 1 - 2 * pp)
        xx = ppx + c * (COLS - 1 - 2 * ppx)
        return {"seq": (zz * COLS + xx) * 2 + c}

    partner = {"seq": place + 1 - 2 * c}

    def row_place(start, off):
        return lax.rem(start + off, COLS)

    barrier = pltpu.get_barrier_semaphore()

    def greet(peer):
        pl.semaphore_signal(barrier, inc=1, device_id=peer, device_id_type=pl.DeviceIdType.MESH)

    greet(partner)
    for off in (1, 2, 3):
        greet({"seq": (z * COLS + row_place(x, off)) * 2 + 1})
    first = lax.rem(z, HALF)
    for d in range(HALF):
        @pl.when(d > first)
        def _():
            zz = z - first + d
            greet({"seq": (zz * COLS + x) * 2 + c})

    for low, high, core in ((0, 7, 0), (0, 6, 0), (3, 4, 0), (3, 5, 0), (0, 7, 1), (1, 7, 1), (3, 4, 1), (2, 4, 1), (3, 6, 0), (1, 4, 1)):
        @pl.when((z == low) & (c == core))
        def _():
            greet({"seq": (high * COLS + x) * 2 + core})

    sources = (k_hbm, v_hbm, q_hbm, g_hbm)
    other_px = COLS - 1 - px

    def load(source, a, j, u):
        return pltpu.make_async_copy(source.at[j, u], inb.at[a, j, u], in_sem.at[a, j, u])

    for core in range(2):
        @pl.when(c == core)
        def _():
            for kind, begin in ((1 - core, other_px), (core, px)):
                for u in range(PER):
                    for off in (2, 1, 3, 0):
                        for a in (2 * kind, 2 * kind + 1):
                            load(sources[a], a, row_place(begin, off), u).start()

    upper = lax.div(z, HALF)
    late_end = jnp.where(z == 7, 2, 0) + jnp.where(z == 4, 3, 0)
    column = upper + jnp.where(z == 6, 1, 0)
    expected = 1 + first + jnp.where(c == 0, column, 6 + late_end)

    def remote(src, dst, send, recv, peer):
        return pltpu.make_async_remote_copy(
            src_ref=src, dst_ref=dst, send_sem=send, recv_sem=recv, device_id=peer,
            device_id_type=pl.DeviceIdType.MESH,
        )

    def core_copy(j, u):
        return remote(away.at[j, u], core_in.at[j, u], ci_s.at[j, u], ci_r.at[j, u], partner)

    def row_copy(off, u):
        j = row_place(px, off)
        return remote(chip.at[j, u], row_in.at[px, u], ri_s.at[off, u], ri_r.at[px, u], device(p, j))

    def pair_copy(d, u):
        return remote(pair_src.at[u], col_in.at[1, u], z_s.at[d, u], z_r.at[1, u], device(g * HALF + d, px))

    def col_copy(d, u):
        return remote(rowsum.at[u], col_in.at[i, u], z_s.at[d, u], z_r.at[i, u], device(g * HALF + d, px))

    def half_copy(to, n, u):
        return remote(half_src.at[u], half_in.at[u], h_s.at[n, u], h_r.at[u], device(to, px))

    def row_back(off, u):
        j = row_place(px, off)
        return remote(row_src.at[off, u], row_out.at[px, u], ro_s.at[off, u], ro_r.at[px, u], device(p, j))

    def core_back(j, u):
        return remote(core_src.at[j, u], core_out.at[j, u], co_s.at[j, u], co_r.at[j, u], partner)

    def arrival(ref, sem):
        return remote(ref, ref, sem, sem, partner)

    def states(kind, begin, into):
        places = [(row_place(begin, off), u) for u in range(PER) for off in (2, 1, 3, 0)]
        for j, u in places:
            for a in (2 * kind, 2 * kind + 1):
                load(k_hbm, a, j, u).wait()
        for j, u in places:
            into[j, u] = dot(inb[2 * kind, j, u], inb[2 * kind + 1, j, u], TN)

    states(1 - c, other_px, away)
    pl.semaphore_wait(barrier, expected)
    for u in range(PER):
        for off in (2, 1, 3, 0):
            core_copy(row_place(other_px, off), u).start()

    @pl.when(c == 1)
    def _():
        pl.semaphore_signal(row_ready, inc=1, device_id=partner, device_id_type=pl.DeviceIdType.MESH)

    states(c, px, own)

    def answer(sender):
        pl.semaphore_signal(
            ready.at[p], inc=1, device_id=device(sender, px), device_id_type=pl.DeviceIdType.MESH
        )

    for s in range(HALF):
        @pl.when((c == 0) & (g == 0) & (s < i))
        def _():
            answer(s)

        @pl.when((c == 1) & (p == 0) & (s > 0))
        def _():
            answer(s)

    @pl.when((c == 0) & (g == 1))
    def _():
        answer(jnp.where(i < 2, HALF - 1, 0))

    @pl.when((c == 0) & (p == 6))
    def _():
        answer(HALF - 1)

    for src, d in ((0, 1), (1, 2), (1, 3), (2, 3)):
        @pl.when((c == 0) & (g == 1) & (i == d))
        def _():
            answer(HALF + src)

    causal = lax.broadcasted_iota(jnp.int32, (tile, tile), 0) >= lax.broadcasted_iota(jnp.int32, (tile, tile), 1)

    def local(half):
        @pl.loop(0, COLS)
        def _(n):
            j, u = half * 2 + lax.div(n, 2), lax.rem(n, 2)
            k, v, q, go = (inb[a, j, u] for a in range(4))
            scores = jnp.where(causal, dot(go, v, NT), 0.0).astype(BF16)
            part[0, j, u] = dot(scores, k, NN)
            part[1, j, u] = dot(scores, q, TN)
            scores = jnp.where(causal, dot(q, k, NT), 0.0).astype(BF16)
            part[2, j, u] = dot(scores, go, TN)

    @pl.when((c == 0) & (g == 1))
    def _():
        local(0)
        local(1)

    @pl.when(c == 0)
    def _():
        pl.semaphore_wait(row_ready, 1)

    for u in range(PER):
        for off in (2, 1, 3, 0):
            j = row_place(px, off)
            core_copy(j, u).wait_recv()
            if off:
                chip[j, u] = own[j, u] + core_in[j, u]
                row_copy(off, u).start()
            else:
                row_in[px, u] = own[px, u] + core_in[px, u]

    def ready_for(d):
        @pl.when((c == 0) == (d > i))
        def _():
            pl.semaphore_wait(ready.at[g * HALF + d], 1)

    def send_column(u, targets):
        for d in targets:
            @pl.when((g == 0) & ((d > i) | ((i > 0) & (d == 0))))
            def _():
                if u == 0:
                    ready_for(d)
                col_copy(d, u).start()

        for src, d in ((0, 1), (2, 3)) if 0 in targets else ():
            @pl.when((g == 1) & (i == src))
            def _():
                if u == 0:
                    ready_for(d)
                col_copy(d, u).start()

    @pl.when((c == 1) | (g == 0))
    def _():
        local(0)

    for u in range(PER):
        for off in (1, 3, 2):
            j = row_place(px, off)
            arrival(row_in.at[j, u], ri_r.at[j, u]).wait_recv()
        total = row_in[0, u]
        ahead[0, u] = jnp.zeros((width, width), F32)
        ahead[1, u] = total
        total = total + row_in[1, u]
        ahead[2, u] = total
        total = total + row_in[2, u]
        ahead[3, u] = total
        rowsum[u] = total + row_in[3, u]

        send_column(u, (0, 3))

    for u in range(PER):
        send_column(u, (2, 1))

    @pl.when((c == 1) & (g == 1))
    def _():
        local(1)


    def row_result(u):
        for off in (2, 1, 3):
            row_src[off, u] = offset[u] + ahead[row_place(px, off), u]
            row_back(off, u).start()
        row_out[px, u] = offset[u] + ahead[px, u]

    def takes(s):
        terms = (i == 1) if s == 0 else (i > 1) if s == 1 else (i == 3)
        return ((g == 0) & (s < i)) | ((g == 1) & terms)

    for u in range(PER):
        offset[u] = jnp.zeros((width, width), F32)
        for s in range(HALF - 1):
            @pl.when(takes(s))
            def _():
                arrival(col_in.at[s, u], z_r.at[s, u]).wait_recv()
                offset[u] += col_in[s, u]

        @pl.when((g == 1) & (i == 1))
        def _():
            pair_src[u] = offset[u] + rowsum[u]
            for d in (3, 2):
                if u == 0:
                    ready_for(d)
                pair_copy(d, u).start()

        @pl.when((g == 0) & (c == 0))
        def _():
            row_result(u)

    for u in range(PER):
        for end, targets in ((0, (7, 6, None)[: 2 - u]), (HALF - 1, (None, 6, 5, 4)[2 - u :])):
            @pl.when((g == 0) & (i == end))
            def _():
                if end == 0:
                    for s in range(1, HALF):
                        arrival(col_in.at[s, u], z_r.at[s, u]).wait_recv()
                    half_src[u] = rowsum[u] + col_in[1, u] + col_in[2, u] + col_in[3, u]
                else:
                    half_src[u] = offset[u] + rowsum[u]
                for n, to in enumerate(targets):
                    if u == 0 or to == 6:
                        @pl.when(c == 0)
                        def _():
                            pl.semaphore_wait(ready.at[to], 1)
                    half_copy(to, n, u).start()

    for u in range(PER):
        @pl.when(g == 1)
        def _():
            arrival(half_in.at[u], h_r.at[u]).wait_recv()
            offset[u] += half_in[u]

        @pl.when((g == 1) | (c == 1))
        def _():
            row_result(u)

    @pl.when(g == 0)
    def _():
        local(1)

    def emit(n, j, u, value):
        (gq, gk, gv)[n][j, u] = (part[n, j, u] + value).astype(BF16)

    def finish(kind, places, states_in):
        @pl.when(kind == 0)
        def _():
            for j, u in places:
                emit(0, j, u, dot(inb[3, j, u], states_in[j, u].astype(BF16), NT))

        @pl.when(kind == 1)
        def _():
            for j, u in places:
                state = states_in[j, u].astype(BF16)
                emit(1, j, u, dot(inb[1, j, u], state, NT))
                emit(2, j, u, dot(inb[0, j, u], state, NN))

    def own_kind():
        for u in range(PER):
            places = [(row_place(px, off), u) for off in (0, 1, 3, 2)]
            for n, (j, _) in enumerate(places):
                if n:
                    arrival(row_out.at[j, u], ro_r.at[j, u]).wait_recv()
                core_src[j, u] = row_out[j, u] + own[j, u]
                core_back(j, u).start()
            finish(c, places, row_out)

    def other_kind():
        for u in range(PER):
            places = [(row_place(other_px, off), u) for off in (0, 1, 3, 2)]
            for batch in (places,) if u == 0 else (places[:3], places[3:]):
                for j, _ in batch:
                    core_back(j, u).wait_recv()
                finish(1 - c, batch, core_out)

    @pl.when(g == 1)
    def _():
        other_kind()

    own_kind()

    @pl.when(g == 0)
    def _():
        other_kind()

    for u in range(PER):
        for off in (1, 2, 3):
            row_copy(off, u).wait_send()
            row_back(off, u).wait_send()
        for d in range(HALF):
            back = (i > 0) if d == 0 else (i == 0) if d == 1 else (i == 1) if d == 2 else (i == 1) | (i == 2)
            forward = (d > i) | ((i > 0) & (d == 0))
            @pl.when(((g == 0) & forward) | ((g == 1) & back & (d > 0)))
            def _():
                col_copy(d, u).wait_send()

        for end, count in ((0, 2 - u), (HALF - 1, 2 + u)):
            @pl.when((g == 0) & (i == end))
            def _():
                for n in range(count):
                    half_copy(0, n, u).wait_send()

        for j in range(COLS):
            core_copy(j, u).wait_send()
            core_back(j, u).wait_send()


def put(*refs):
    sources, targets, sems = refs[:3], refs[3:6], refs[6]
    copies = [
        pltpu.make_async_copy(sources[n].at[j], targets[n].at[j], sems.at[n, j])
        for n in range(3)
        for j in range(COLS)
    ]
    for copy in copies:
        copy.start()
    for copy in copies:
        copy.wait()


def body(queries, key_rows, value_rows, grad_out):
    heads, tile, width = queries.shape
    split = (COLS, PER, tile, width)
    square = (width, width)
    sem = pltpu.SemaphoreType.DMA
    four = pltpu.VMEM((COLS, PER, *square), F32)
    two = pltpu.VMEM((PER, *square), F32)
    pairs = sem((COLS, PER))
    grads = pl.pallas_call(
        kernel,
        out_shape=[pltpu.VMEM(split, BF16)] * 3,
        in_specs=[pl.BlockSpec(memory_space=pl.ANY)] * 4,
        out_specs=[pl.BlockSpec(memory_space=pltpu.VMEM)] * 3,
        scratch_shapes=[
            pltpu.VMEM((4, *split), BF16),
            pltpu.VMEM((3, *split), F32),
            four, four, four, four, four, four, two, four, two, two, two, two,
            four, four, four, four,
            sem((4, COLS, PER)),
            pairs, pairs, pairs, pairs, pairs, pairs, sem((3, PER)), sem((PER,)), pairs, pairs, pairs, pairs,
            pltpu.SemaphoreType.REGULAR((ROWS,)),
            pltpu.SemaphoreType.REGULAR,
        ],
        compiler_params=pltpu.CompilerParams(
            collective_id=0, has_side_effects=True, vmem_limit_bytes=61 * 2**20
        ),
    )(*(a.reshape(split) for a in (key_rows, value_rows, queries, grad_out)))
    grads = pl.pallas_call(
        put,
        out_shape=[jax.ShapeDtypeStruct(split, BF16)] * 3,
        in_specs=[pl.BlockSpec(memory_space=pl.ANY)] * 3,
        out_specs=[pl.BlockSpec(memory_space=pl.ANY)] * 3,
        scratch_shapes=[sem((3, COLS))],
        compiler_params=pltpu.CompilerParams(vmem_limit_bytes=2**20),
    )(*grads)
    return tuple(a.reshape(heads, tile, width) for a in grads)


def solution(mesh):
    placed = P("head", "seq", None)
    return jax.shard_map(
        body, mesh=mesh, in_specs=(placed,) * 4, out_specs=(placed,) * 3, check_vma=False
    )
```

time: 38.6 us -> 34 us (0.88)
  Pallas kernels: 37.9 us -> 33.1 us
    pallas_call x1, Pallas kernels: 36.6 us -> 31.9 us  [body(): pl.pallas_call(kernel, out_shape=[pltpu.VMEM(split, BF16)] * 3, in_specs=...]
where the time goes in v3:
time: 34 us; the launch traced here: 33.8 us
  Pallas kernels  33.1 us (97%)
  between operations  0.64 us (2%)
    pallas_call x1, Pallas kernels, body(): pl.pallas_call(kernel, out_shape=[pltpu.VMEM(split, BF16)] * 3, in_specs=...  31.9 us
    pallas_call x1, Pallas kernels, body(): pl.pallas_call(put, out_shape=[jax.ShapeDtypeStruct(split, BF16)] * 3, in...  1.24 us

profile of v3, /device:TPU:1, one launch (start us, length us, event | category | flops | bytes accessed | tf_op | source)
XLA Modules:
  0.0 33.8 jit_solution(16678676149347320009)
XLA Ops:
  0.6 31.9 %shard_map.67 = (bf16[4,2,256,128]{3,2,1,0:T(8,128)(2,1)S(1)}, bf16[4,2,256,128]{3,2,1,0:T(8,128)(2,1)S(1)}, bf16[4,2,256,128]{3,2,1,0:T(8,128)(2,1)S(1)}) custom-call(bf16[4,2,256,128]{3,2,1,0:T(8,128)(2,1)} %bitcast.7, bf16[4,2,256,128]{3,2,1,0:T(8,128)(2,1)} %bitcast.8, bf16[4,2,256,128]{3,2,1,0:T(8,128)(2,1)} %bitcast.9, bf16[4,2,256,128]{3,2,1,0:T(8,128)(2,1)} %bitcast.10), custom_call_target="tpu_custom_call" | custom-call | tf_op jit(solution)/shard_map/pallas_call | solution.py:394
  32.5 1.2 %shard_map.68 = (bf16[4,2,256,128]{3,2,1,0:T(8,128)(2,1)}, bf16[4,2,256,128]{3,2,1,0:T(8,128)(2,1)}, bf16[4,2,256,128]{3,2,1,0:T(8,128)(2,1)}) custom-call(bf16[4,2,256,128]{3,2,1,0:T(8,128)(2,1)S(1)} %get-tuple-element.9.refs_0_, bf16[4,2,256,128]{3,2,1,0:T(8,128)(2,1)S(1)} %get-tuple-element.10.refs_1_, bf16[4,2,256,128]{3,2,1,0:T(8,128)(2,1)S(1)} %get-tuple-element.11.refs_2_), custom_call_target="tpu_custom_call" | custom-call | tf_op jit(solution)/shard_map/pallas_call | solution.py:413

commit v4 on v3

--- a/solution.py
+++ b/solution.py
@@ -68,17 +68,11 @@
     sources = (k_hbm, v_hbm, q_hbm, g_hbm)
     other_px = COLS - 1 - px
 
-    def load(source, a, j, u):
-        return pltpu.make_async_copy(source.at[j, u], inb.at[a, j, u], in_sem.at[a, j, u])
-
-    for core in range(2):
-        @pl.when(c == core)
-        def _():
-            for kind, begin in ((1 - core, other_px), (core, px)):
-                for u in range(PER):
-                    for off in (2, 1, 3, 0):
-                        for a in (2 * kind, 2 * kind + 1):
-                            load(sources[a], a, row_place(begin, off), u).start()
+    def load(source, a):
+        return pltpu.make_async_copy(source, inb.at[a], in_sem.at[a])
+
+    for a in (2, 3, 0, 1):
+        load(sources[a], a).start()
 
     upper = lax.div(z, HALF)
     late_end = jnp.where(z == 7, 2, 0) + jnp.where(z == 4, 3, 0)
@@ -92,50 +86,57 @@
         )
 
     def core_copy(j, u):
-        return remote(away.at[j, u], core_in.at[j, u], ci_s.at[j, u], ci_r.at[j, u], partner)
+        return remote(away.at[j, u], core_in.at[j, u], ci_s, ci_r.at[j, u], partner)
 
     def row_copy(off, u):
         j = row_place(px, off)
-        return remote(chip.at[j, u], row_in.at[px, u], ri_s.at[off, u], ri_r.at[px, u], device(p, j))
+        return remote(chip.at[j, u], row_in.at[px, u], ri_s, ri_r.at[u], device(p, j))
 
     def pair_copy(d, u):
-        return remote(pair_src.at[u], col_in.at[1, u], z_s.at[d, u], z_r.at[1, u], device(g * HALF + d, px))
+        return remote(pair_src.at[u], col_in.at[1, u], z_s.at[d], z_r.at[1, u], device(g * HALF + d, px))
 
     def col_copy(d, u):
-        return remote(rowsum.at[u], col_in.at[i, u], z_s.at[d, u], z_r.at[i, u], device(g * HALF + d, px))
-
-    def half_copy(to, n, u):
-        return remote(half_src.at[u], half_in.at[u], h_s.at[n, u], h_r.at[u], device(to, px))
+        return remote(rowsum.at[u], col_in.at[i, u], z_s.at[d], z_r.at[i, u], device(g * HALF + d, px))
+
+    def half_copy(to, u):
+        return remote(half_src.at[u], half_in.at[u], h_s.at[u], h_r.at[u], device(to, px))
 
     def row_back(off, u):
         j = row_place(px, off)
-        return remote(row_src.at[off, u], row_out.at[px, u], ro_s.at[off, u], ro_r.at[px, u], device(p, j))
-
-    def core_back(j, u):
-        return remote(core_src.at[j, u], core_out.at[j, u], co_s.at[j, u], co_r.at[j, u], partner)
+        return remote(row_src.at[off, u], row_out.at[px, u], ro_s, ro_r.at[px, u], device(p, j))
+
+    def core_back(j, u, off):
+        batch = u + 1 if u == 1 and off == 2 else u
+        return remote(core_src.at[j, u], core_out.at[j, u], co_s, co_r.at[batch], partner)
 
     def arrival(ref, sem):
         return remote(ref, ref, sem, sem, partner)
 
     def states(kind, begin, into):
         places = [(row_place(begin, off), u) for u in range(PER) for off in (2, 1, 3, 0)]
-        for j, u in places:
-            for a in (2 * kind, 2 * kind + 1):
-                load(k_hbm, a, j, u).wait()
+        for a in (2 * kind, 2 * kind + 1):
+            load(k_hbm, a).wait()
         for j, u in places:
             into[j, u] = dot(inb[2 * kind, j, u], inb[2 * kind + 1, j, u], TN)
 
-    states(1 - c, other_px, away)
-    pl.semaphore_wait(barrier, expected)
-    for u in range(PER):
-        for off in (2, 1, 3, 0):
-            core_copy(row_place(other_px, off), u).start()
+    def hand_in():
+        pl.semaphore_wait(barrier, expected)
+        for u in range(PER):
+            for off in (2, 1, 3, 0):
+                core_copy(row_place(other_px, off), u).start()
+
+    @pl.when(c == 0)
+    def _():
+        states(1, other_px, away)
+        hand_in()
+        states(0, px, own)
 
     @pl.when(c == 1)
     def _():
+        states(1, px, own)
+        states(0, other_px, away)
+        hand_in()
         pl.semaphore_signal(row_ready, inc=1, device_id=partner, device_id_type=pl.DeviceIdType.MESH)
-
-    states(c, px, own)
 
     def answer(sender):
         pl.semaphore_signal(
@@ -221,9 +222,7 @@
         local(0)
 
     for u in range(PER):
-        for off in (1, 3, 2):
-            j = row_place(px, off)
-            arrival(row_in.at[j, u], ri_r.at[j, u]).wait_recv()
+        arrival(row_in.at[pl.ds(0, 3), u], ri_r.at[u]).wait_recv()
         total = row_in[0, u]
         ahead[0, u] = jnp.zeros((width, width), F32)
         ahead[1, u] = total
@@ -274,7 +273,7 @@
             row_result(u)
 
     for u in range(PER):
-        for end, targets in ((0, (7, 6, None)[: 2 - u]), (HALF - 1, (None, 6, 5, 4)[2 - u :])):
+        for end, due in ((0, ([(7, 0)], [(7, 1), (6, 1)])), (HALF - 1, ([(6, 0), (5, 0)], [(5, 1), (4, 0), (4, 1)]))):
             @pl.when((g == 0) & (i == end))
             def _():
                 if end == 0:
@@ -283,12 +282,12 @@
                     half_src[u] = rowsum[u] + col_in[1, u] + col_in[2, u] + col_in[3, u]
                 else:
                     half_src[u] = offset[u] + rowsum[u]
-                for n, to in enumerate(targets):
-                    if u == 0 or to == 6:
+                for to, which in due[u]:
+                    if which == 0 or to == 6:
                         @pl.when(c == 0)
                         def _():
                             pl.semaphore_wait(ready.at[to], 1)
-                    half_copy(to, n, u).start()
+                    half_copy(to, which).start()
 
     for u in range(PER):
         @pl.when(g == 1)
@@ -323,19 +322,19 @@
     def own_kind():
         for u in range(PER):
             places = [(row_place(px, off), u) for off in (0, 1, 3, 2)]
-            for n, (j, _) in enumerate(places):
-                if n:
+            for off, (j, _) in zip((0, 1, 3, 2), places):
+                if off:
                     arrival(row_out.at[j, u], ro_r.at[j, u]).wait_recv()
                 core_src[j, u] = row_out[j, u] + own[j, u]
-                core_back(j, u).start()
+                core_back(j, u, off).start()
             finish(c, places, row_out)
 
     def other_kind():
         for u in range(PER):
             places = [(row_place(other_px, off), u) for off in (0, 1, 3, 2)]
             for batch in (places,) if u == 0 else (places[:3], places[3:]):
-                for j, _ in batch:
-                    core_back(j, u).wait_recv()
+                last = u + 1 if len(batch) == 1 else u
+                arrival(core_out.at[pl.ds(0, len(batch)), u], co_r.at[last]).wait_recv()
                 finish(1 - c, batch, core_out)
 
     @pl.when(g == 1)
@@ -348,34 +347,37 @@
     def _():
         other_kind()
 
-    for u in range(PER):
-        for off in (1, 2, 3):
-            row_copy(off, u).wait_send()
-            row_back(off, u).wait_send()
-        for d in range(HALF):
-            back = (i > 0) if d == 0 else (i == 0) if d == 1 else (i == 1) if d == 2 else (i == 1) | (i == 2)
-            forward = (d > i) | ((i > 0) & (d == 0))
-            @pl.when(((g == 0) & forward) | ((g == 1) & back & (d > 0)))
-            def _():
-                col_copy(d, u).wait_send()
-
-        for end, count in ((0, 2 - u), (HALF - 1, 2 + u)):
-            @pl.when((g == 0) & (i == end))
-            def _():
-                for n in range(count):
-                    half_copy(0, n, u).wait_send()
-
-        for j in range(COLS):
-            core_copy(j, u).wait_send()
-            core_back(j, u).wait_send()
+    def sent(ref, sem):
+        remote(ref, ref, sem, sem, partner).wait_send()
+
+    sent(away, ci_s)
+    sent(chip.at[pl.ds(0, 3)], ri_s)
+    sent(row_src.at[pl.ds(1, 3)], ro_s)
+    sent(core_src, co_s)
+    for d in range(HALF):
+        back = ((i == 0) if d == 1 else (i == 1) if d == 2 else (i == 1) | (i == 2)) & (d > 0)
+        forward = (d > i) | ((i > 0) & (d == 0))
+
+        @pl.when(((g == 0) & forward) | ((g == 1) & back))
+        def _():
+            sent(rowsum, z_s.at[d])
+
+    @pl.when((g == 0) & (i == 0))
+    def _():
+        sent(half_src.at[0], h_s.at[0])
+        sent(half_src, h_s.at[1])
+
+    @pl.when((g == 0) & (i == HALF - 1))
+    def _():
+        sent(row_src.at[pl.ds(1, 3), 0], h_s.at[0])
+        sent(half_src, h_s.at[1])
 
 
 def put(*refs):
     sources, targets, sems = refs[:3], refs[3:6], refs[6]
     copies = [
-        pltpu.make_async_copy(sources[n].at[j], targets[n].at[j], sems.at[n, j])
+        pltpu.make_async_copy(sources[n], targets[n], sems.at[n])
         for n in range(3)
-        for j in range(COLS)
     ]
     for copy in copies:
         copy.start()
@@ -401,8 +403,8 @@
             pltpu.VMEM((3, *split), F32),
             four, four, four, four, four, four, two, four, two, two, two, two,
             four, four, four, four,
-            sem((4, COLS, PER)),
-            pairs, pairs, pairs, pairs, pairs, pairs, sem((3, PER)), sem((PER,)), pairs, pairs, pairs, pairs,
+            sem((4,)),
+            sem, pairs, sem, sem((PER,)), sem((COLS,)), pairs, sem((PER,)), sem((PER,)), sem, pairs, sem, sem((PER + 1,)),
             pltpu.SemaphoreType.REGULAR((ROWS,)),
             pltpu.SemaphoreType.REGULAR,
         ],
@@ -415,7 +417,7 @@
         out_shape=[jax.ShapeDtypeStruct(split, BF16)] * 3,
         in_specs=[pl.BlockSpec(memory_space=pl.ANY)] * 3,
         out_specs=[pl.BlockSpec(memory_space=pl.ANY)] * 3,
-        scratch_shapes=[sem((3, COLS))],
+        scratch_shapes=[sem((3,))],
         compiler_params=pltpu.CompilerParams(vmem_limit_bytes=2**20),
     )(*grads)
     return tuple(a.reshape(heads, tile, width) for a in grads)

time: 34 us -> 32.8 us (0.965)
  Pallas kernels: 33.1 us -> 32 us
    pallas_call x1, Pallas kernels: 31.9 us -> 30.8 us  [body(): pl.pallas_call(kernel, out_shape=[pltpu.VMEM(split, BF16)] * 3, in_specs=...]
where the time goes in v4:
time: 32.8 us; the launch traced here: 32.6 us
  Pallas kernels  32 us (98%)
  between operations  0.64 us (2%)
    pallas_call x1, Pallas kernels, body(): pl.pallas_call(kernel, out_shape=[pltpu.VMEM(split, BF16)] * 3, in_specs=...  30.8 us
    pallas_call x1, Pallas kernels, body(): pl.pallas_call(put, out_shape=[jax.ShapeDtypeStruct(split, BF16)] * 3, in...  1.17 us

profile of v4, /device:TPU:1, one launch (start us, length us, event | category | flops | bytes accessed | tf_op | source)
XLA Modules:
  0.0 32.6 jit_solution(446472435916524748)
XLA Ops:
  0.6 30.8 %shard_map.67 = (bf16[4,2,256,128]{3,2,1,0:T(8,128)(2,1)S(1)}, bf16[4,2,256,128]{3,2,1,0:T(8,128)(2,1)S(1)}, bf16[4,2,256,128]{3,2,1,0:T(8,128)(2,1)S(1)}) custom-call(bf16[4,2,256,128]{3,2,1,0:T(8,128)(2,1)} %bitcast.7, bf16[4,2,256,128]{3,2,1,0:T(8,128)(2,1)} %bitcast.8, bf16[4,2,256,128]{3,2,1,0:T(8,128)(2,1)} %bitcast.9, bf16[4,2,256,128]{3,2,1,0:T(8,128)(2,1)} %bitcast.10), custom_call_target="tpu_custom_call" | custom-call | tf_op jit(solution)/shard_map/pallas_call | solution.py:396
  31.5 1.2 %shard_map.68 = (bf16[4,2,256,128]{3,2,1,0:T(8,128)(2,1)}, bf16[4,2,256,128]{3,2,1,0:T(8,128)(2,1)}, bf16[4,2,256,128]{3,2,1,0:T(8,128)(2,1)}) custom-call(bf16[4,2,256,128]{3,2,1,0:T(8,128)(2,1)S(1)} %get-tuple-element.9.refs_0_, bf16[4,2,256,128]{3,2,1,0:T(8,128)(2,1)S(1)} %get-tuple-element.10.refs_1_, bf16[4,2,256,128]{3,2,1,0:T(8,128)(2,1)S(1)} %get-tuple-element.11.refs_2_), custom_call_target="tpu_custom_call" | custom-call | tf_op jit(solution)/shard_map/pallas_call | solution.py:415

commit v5 on v4

--- a/solution.py
+++ b/solution.py
@@ -68,11 +68,13 @@
     sources = (k_hbm, v_hbm, q_hbm, g_hbm)
     other_px = COLS - 1 - px
 
-    def load(source, a):
-        return pltpu.make_async_copy(source, inb.at[a], in_sem.at[a])
-
-    for a in (2, 3, 0, 1):
-        load(sources[a], a).start()
+    def load(source, a, u):
+        return pltpu.make_async_copy(source.at[:, u], inb.at[a, :, u], in_sem.at[a, u])
+
+    for pair in ((2, 3), (0, 1)):
+        for u in range(PER):
+            for a in pair:
+                load(sources[a], a, u).start()
 
     upper = lax.div(z, HALF)
     late_end = jnp.where(z == 7, 2, 0) + jnp.where(z == 4, 3, 0)
@@ -112,30 +114,33 @@
     def arrival(ref, sem):
         return remote(ref, ref, sem, sem, partner)
 
-    def states(kind, begin, into):
-        places = [(row_place(begin, off), u) for u in range(PER) for off in (2, 1, 3, 0)]
-        for a in (2 * kind, 2 * kind + 1):
-            load(k_hbm, a).wait()
+    def states(kind, begin, into, which):
+        places = [(row_place(begin, off), u) for u in which for off in (2, 1, 3, 0)]
+        for u in which:
+            for a in (2 * kind, 2 * kind + 1):
+                load(sources[a], a, u).wait()
         for j, u in places:
             into[j, u] = dot(inb[2 * kind, j, u], inb[2 * kind + 1, j, u], TN)
 
-    def hand_in():
-        pl.semaphore_wait(barrier, expected)
-        for u in range(PER):
+    def hand_in(which):
+        if 0 in which:
+            pl.semaphore_wait(barrier, expected)
+        for u in which:
             for off in (2, 1, 3, 0):
                 core_copy(row_place(other_px, off), u).start()
 
     @pl.when(c == 0)
     def _():
-        states(1, other_px, away)
-        hand_in()
-        states(0, px, own)
+        for u in range(PER):
+            states(1, other_px, away, (u,))
+            hand_in((u,))
+        states(0, px, own, (0, 1))
 
     @pl.when(c == 1)
     def _():
-        states(1, px, own)
-        states(0, other_px, away)
-        hand_in()
+        states(1, px, own, (0, 1))
+        states(0, other_px, away, (0, 1))
+        hand_in((0, 1))
         pl.semaphore_signal(row_ready, inc=1, device_id=partner, device_id_type=pl.DeviceIdType.MESH)
 
     def answer(sender):
@@ -160,7 +165,7 @@
     def _():
         answer(HALF - 1)
 
-    for src, d in ((0, 1), (1, 2), (1, 3), (2, 3)):
+    for src, d in ((0, 1), (0, 2), (1, 2), (1, 3), (2, 3)):
         @pl.when((c == 0) & (g == 1) & (i == d))
         def _():
             answer(HALF + src)
@@ -210,8 +215,8 @@
                     ready_for(d)
                 col_copy(d, u).start()
 
-        for src, d in ((0, 1), (2, 3)) if 0 in targets else ():
-            @pl.when((g == 1) & (i == src))
+        for src, d in ((0, 1), (0, 2), (1, 2), (2, 3)) if 0 in targets else ():
+            @pl.when((g == 1) & (i == src) & ((c == 0) | (d != 2)))
             def _():
                 if u == 0:
                     ready_for(d)
@@ -249,7 +254,7 @@
         row_out[px, u] = offset[u] + ahead[px, u]
 
     def takes(s):
-        terms = (i == 1) if s == 0 else (i > 1) if s == 1 else (i == 3)
+        terms = (i == 1) | ((i == 2) & (c == 0)) if s == 0 else (i > 1) if s == 1 else (i == 3)
         return ((g == 0) & (s < i)) | ((g == 1) & terms)
 
     for u in range(PER):
@@ -263,10 +268,13 @@
         @pl.when((g == 1) & (i == 1))
         def _():
             pair_src[u] = offset[u] + rowsum[u]
-            for d in (3, 2):
-                if u == 0:
-                    ready_for(d)
-                pair_copy(d, u).start()
+            if u == 0:
+                ready_for(3)
+            pair_copy(3, u).start()
+
+            @pl.when(c == 1)
+            def _():
+                pair_copy(2, u).start()
 
         @pl.when((g == 0) & (c == 0))
         def _():
@@ -355,7 +363,7 @@
     sent(row_src.at[pl.ds(1, 3)], ro_s)
     sent(core_src, co_s)
     for d in range(HALF):
-        back = ((i == 0) if d == 1 else (i == 1) if d == 2 else (i == 1) | (i == 2)) & (d > 0)
+        back = ((i == 0) if d == 1 else (i == 1) | ((i == 0) & (c == 0)) if d == 2 else (i == 1) | (i == 2)) & (d > 0)
         forward = (d > i) | ((i > 0) & (d == 0))
 
         @pl.when(((g == 0) & forward) | ((g == 1) & back))
@@ -403,7 +411,7 @@
             pltpu.VMEM((3, *split), F32),
             four, four, four, four, four, four, two, four, two, two, two, two,
             four, four, four, four,
-            sem((4,)),
+            sem((4, PER)),
             sem, pairs, sem, sem((PER,)), sem((COLS,)), pairs, sem((PER,)), sem((PER,)), sem, pairs, sem, sem((PER + 1,)),
             pltpu.SemaphoreType.REGULAR((ROWS,)),
             pltpu.SemaphoreType.REGULAR,

time: 32.8 us -> 32.8 us (level)
  no operation moved by 1% of the time
where the time goes in v5:
time: 32.8 us; the launch traced here: 32.6 us
  Pallas kernels  32 us (98%)
  between operations  0.64 us (2%)
    pallas_call x1, Pallas kernels, body(): pl.pallas_call(kernel, out_shape=[pltpu.VMEM(split, BF16)] * 3, in_specs=...  30.8 us
    pallas_call x1, Pallas kernels, body(): pl.pallas_call(put, out_shape=[jax.ShapeDtypeStruct(split, BF16)] * 3, in...  1.17 us

profile of v5, /device:TPU:1, one launch (start us, length us, event | category | flops | bytes accessed | tf_op | source)
XLA Modules:
  0.0 32.6 jit_solution(6794249669256464246)
XLA Ops:
  0.6 30.8 %shard_map.67 = (bf16[4,2,256,128]{3,2,1,0:T(8,128)(2,1)S(1)}, bf16[4,2,256,128]{3,2,1,0:T(8,128)(2,1)S(1)}, bf16[4,2,256,128]{3,2,1,0:T(8,128)(2,1)S(1)}) custom-call(bf16[4,2,256,128]{3,2,1,0:T(8,128)(2,1)} %bitcast.7, bf16[4,2,256,128]{3,2,1,0:T(8,128)(2,1)} %bitcast.8, bf16[4,2,256,128]{3,2,1,0:T(8,128)(2,1)} %bitcast.9, bf16[4,2,256,128]{3,2,1,0:T(8,128)(2,1)} %bitcast.10), custom_call_target="tpu_custom_call" | custom-call | tf_op jit(solution)/shard_map/pallas_call | solution.py:404
  31.5 1.2 %shard_map.68 = (bf16[4,2,256,128]{3,2,1,0:T(8,128)(2,1)}, bf16[4,2,256,128]{3,2,1,0:T(8,128)(2,1)}, bf16[4,2,256,128]{3,2,1,0:T(8,128)(2,1)}) custom-call(bf16[4,2,256,128]{3,2,1,0:T(8,128)(2,1)S(1)} %get-tuple-element.9.refs_0_, bf16[4,2,256,128]{3,2,1,0:T(8,128)(2,1)S(1)} %get-tuple-element.10.refs_1_, bf16[4,2,256,128]{3,2,1,0:T(8,128)(2,1)S(1)} %get-tuple-element.11.refs_2_), custom_call_target="tpu_custom_call" | custom-call | tf_op jit(solution)/shard_map/pallas_call | solution.py:423
